TPU v7x, 512 devices: a whole 4x8x8 slice. The times are simulated.
512 devices in a mesh: bin: 64 (over z, x, y_hi), grp: 8 (over y_lo, core).
Axes of the slice: x: 4, y: 8 (y_hi: 2, y_lo: 4; y = y_hi * 4 + y_lo), z: 8, core: 2. Of those that a mesh axis runs over, the one named last changes fastest.
Arguments:
- record: bfloat16 [8, 256, 8704], P('grp', 'bin'), may hold values from -60 to 60
- ref_index: int32 [8, 16], P('grp'), may hold values from 0 to 255, as said below
- offsets: int32 [16], replicated, may hold values from 0 to 7680, as said below
Outputs:
- transfer: bfloat16 [512, 2048, 256], P('bin', 'grp')
Inputs may be any that keep to these rules, and one draw needn't show every extreme that they name: `ref_index`: each row lists 16 different channels of its group; every row holds 0 and 255. `offsets`: starts rise; the first is 0, the last is 7680, and neighbours lie 512 // 2 to 768 apart.
All inputs are finite; a program needn't handle non-finite values.
Results may differ from a plain program's by a relative error of at most 0.0095.
Values may be sent and summed in bfloat16 or wider, within the bound.
A program may use at most 64 MiB of HBM per device.

v0:
```python
import math
import jax
import jax.numpy as jnp
from jax import lax
from jax.sharding import PartitionSpec as P

L = 1024
NB = 512
ridge_weight = 0.5


def make_table(seg_len, bins):
    sample_num = lax.iota(jnp.int32, seg_len)[:, None]
    bin_num = lax.iota(jnp.int32, bins)[None, :]
    angles = (sample_num * bin_num % seg_len).astype(jnp.float32) * (2.0 * math.pi / seg_len)
    hann_window = 0.5 - 0.5 * jnp.cos(sample_num.astype(jnp.float32) * (2.0 * math.pi / seg_len))
    return jnp.concatenate(
        [hann_window * jnp.cos(angles), -(hann_window * jnp.sin(angles))], axis=1
    ).astype(jnp.bfloat16)


def transform(chan_rows, starts, dft_table, bin_devices):
    seg_len = dft_table.shape[0]
    pieces = jax.vmap(lambda start_at: lax.dynamic_slice_in_dim(chan_rows, start_at, seg_len, 1))(
        starts
    )
    spectra = jnp.einsum(
        "scn,nk->ksc", pieces, dft_table, preferred_element_type=jnp.float32
    ).astype(jnp.bfloat16)
    bin_total = dft_table.shape[1] // 2
    return spectra.reshape(
        2, bin_devices, bin_total // bin_devices, starts.shape[0], chan_rows.shape[0]
    )


def local(record, ref_index, offsets):
    chan_rows = record[0]
    dft_table = make_table(L, NB)
    bin_devices = lax.axis_size("bin")
    spectra = transform(chan_rows, offsets, dft_table, bin_devices)
    channels = lax.all_to_all(spectra, "bin", split_axis=1, concat_axis=4, tiled=True)[:, 0]
    local_refs = jnp.take(channels, ref_index[0], axis=3)
    references = lax.all_gather(local_refs, "grp", axis=3, tiled=True)
    ref_real = references[0]
    ref_imag = references[1]
    ref_blocks = jnp.stack(
        [
            jnp.concatenate([ref_real, -ref_imag], axis=-1),
            jnp.concatenate([ref_imag, ref_real], axis=-1),
        ]
    )
    bins_here = channels.shape[1]
    group_size = math.gcd(bins_here, 4)
    group_count = bins_here // group_size
    real_order = ref_blocks.shape[-1]

    def solve_group(group_index):
        first_bin = group_index * group_size
        ref_group = lax.dynamic_slice_in_dim(ref_blocks, first_bin, group_size, 1)
        chan_group = lax.dynamic_slice_in_dim(channels, first_bin, group_size, 1)
        cross_part = jnp.einsum(
            "pfsr,pfsc->frc", ref_group, chan_group, preferred_element_type=jnp.float32
        )
        auto_part = jnp.einsum(
            "pfsr,pfsq->frq", ref_group, ref_group, preferred_element_type=jnp.float32
        )
        ridge_term = ridge_weight * jnp.trace(auto_part, axis1=1, axis2=2) / real_order
        factor = jnp.linalg.cholesky(
            auto_part + ridge_term[:, None, None] * jnp.eye(real_order, dtype=jnp.float32)
        )
        transfer_t = jax.scipy.linalg.cho_solve((factor, True), cross_part)
        return jnp.swapaxes(transfer_t, 1, 2).astype(jnp.bfloat16)

    results = lax.map(solve_group, jnp.arange(group_count))
    return results.reshape(bins_here, results.shape[2], results.shape[3])


def solution(mesh):
    placed = (P("grp", "bin", None), P("grp", None), P())
    return jax.shard_map(
        local, mesh=mesh, in_specs=placed, out_specs=P("bin", "grp", None), check_vma=False
    )
```

profile of v0, /device:TPU:1, one launch (start us, length us, event | category | flops | bytes accessed | tf_op | source)
XLA Modules:
  0.0 550.2 jit_solution(7552281096765540275)
XLA Ops:
  0.1 8.9 %multiply_convert_fusion = (bf16[1024,512]{1,0:T(8,128)(2,1)S(1)}, bf16[1024,512]{1,0:T(8,128)(2,1)S(1)}) fusion(f32[1024]{0:T(1024)S(1)} %multiply_subtract_fusion), kind=kLoop, calls=%fused_computation.58 | loop fusion | flops 9961472 | bytes 2101248 | tf_op jit(solution)/shard_map/convert.2
  9.0 32.3 %while.17 = (s32[]{:T(128)}, bf16[4,8704]{1,0:T(4,128)(2,1)}, s32[16,2]{0,1:T(2,128)S(1)}, bf16[16,4,1024]{2,1,0:T(4,128)(2,1)S(1)}, s32[]{:T(128)}) while((s32[]{:T(128)}, bf16[4,8704]{1,0:T(4,128)(2,1)}, s32[16,2]{0,1:T(2,128)S(1)}, bf16[16,4,1024]{2,1,0:T(4,128)(2,1)S(1)}, s32[]{:T(128)}) %tuple.87), condition=%wide.while_cond.1, body=%wide.while_body.1.sunk | while | flops 2 | bytes 16481 | solution.py:24
  9.6 1.4 bitcast_dynamic-update-slice_fusion.4
  11.6 1.4 bitcast_dynamic-update-slice_fusion.4
  13.6 1.4 bitcast_dynamic-update-slice_fusion.4
  15.7 1.4 bitcast_dynamic-update-slice_fusion.4
  17.7 1.4 bitcast_dynamic-update-slice_fusion.4
  19.7 1.4 bitcast_dynamic-update-slice_fusion.4
  21.7 1.4 bitcast_dynamic-update-slice_fusion.4
  23.7 1.4 bitcast_dynamic-update-slice_fusion.4
  25.7 1.4 bitcast_dynamic-update-slice_fusion.4
  27.7 1.4 bitcast_dynamic-update-slice_fusion.4
  29.8 1.4 bitcast_dynamic-update-slice_fusion.4
  31.8 1.4 bitcast_dynamic-update-slice_fusion.4
  33.8 1.4 bitcast_dynamic-update-slice_fusion.4
  35.8 1.4 bitcast_dynamic-update-slice_fusion.4
  39.8 1.4 bitcast_dynamic-update-slice_fusion.4
  42.5 1.8 reshape.166
  44.3 19.6 %all-to-all-start = ((bf16[64,2,512]{2,1,0:T(2,128)(2,1)}), bf16[64,2,512]{2,1,0:T(2,128)(2,1)S(1)}, u32[]{:S(2)}, u32[]{:S(2)}) async-start(bf16[64,2,512]{2,1,0:T(2,128)(2,1)} %reshape.166), calls=%async_computation | async-start | bytes 262144 | tf_op jit(solution)/shard_map/all_to_all | solution.py:41
  63.9 13.6 %all-to-all-done = bf16[64,2,512]{2,1,0:T(2,128)(2,1)S(1)} async-done(((bf16[64,2,512]{2,1,0:T(2,128)(2,1)}), bf16[64,2,512]{2,1,0:T(2,128)(2,1)S(1)}, u32[]{:S(2)}, u32[]{:S(2)}) %all-to-all-start) | async-done | bytes 131104 | tf_op jit(solution)/shard_map/all_to_all | solution.py:41
  79.2 16.7 %all_gather.3 = bf16[2,8,16,128]{2,1,0,3:T(8,128)(2,1)S(1)} all-gather(bf16[2,8,16,16]{2,1,0,3:T(8,128)(2,1)S(1)} %select_bitcast_fusion.1), channel_id=1, replica_groups=mesh['bin'=64,'grp'=8] {'grp'}, dimensions={3}, use_global_device_ids=true | all-gather | bytes 73728 | tf_op jit(solution)/shard_map/all_gather | solution.py:43
  97.5 452.7 %while.16 = (s32[]{:T(128)}, bf16[2,4,256,256]{3,2,1,0:T(8,128)(2,1)}, s32[2]{0:T(128)S(1)}, bf16[2,8,16,256]{3,2,1,0:T(8,128)(2,1)S(1)}, bf16[2,8,16,256]{3,2,0...) while((s32[]{:T(128)}, ...), condition=%wide.region_6.7_spmd, body=%wide.region_0.6_spmd.sunk | while | flops 1448117248 | bytes 37234176 | solution.py:74
  100.1 46.9 %custom-call.42 = f32[4,128,128]{2,1,0:T(8,128)S(1)} custom-call(f32[4,128,128]{2,1,0:T(8,128)S(1)} %cholesky.172), custom_call_target="Cholesky" | custom-call | tf_op jit(solution)/shard_map/while/body/eval_jaxpr/jit(cholesky)/cholesky | solution.py:68
  147.1 39.3 %custom-call.43 = f32[4,1,128,128]{2,3,1,0:T(8,128)S(1)} custom-call(f32[4,1,128,128]{3,2,1,0:T(8,128)S(1)} %select_bitcast_fusion.3), custom_call_target="InvertDiagBlocksLowerTriangular" | custom-call | tf_op jit(solution)/shard_map/while/body/eval_jaxpr/jit(cholesky)/cholesky | solution.py:68
  187.5 46.9 %custom-call.44 = f32[4,128,128]{2,1,0:T(8,128)S(1)} custom-call(f32[4,128,128]{2,1,0:T(8,128)S(1)} %convolution_subtract_fusion.6), custom_call_target="Cholesky" | custom-call | tf_op jit(solution)/shard_map/while/body/eval_jaxpr/jit(cholesky)/cholesky | solution.py:68
  235.1 3.9 while.18
  239.0 78.6 %custom-call.46 = f32[4,2,128,128]{2,3,1,0:T(8,128)S(1)} custom-call(f32[4,2,128,128]{3,2,1,0:T(8,128)S(1)} %bitcast.144), custom_call_target="InvertDiagBlocksLowerTriangular" | custom-call | tf_op jit(solution)/shard_map/while/body/eval_jaxpr/jit(_cho_solve)/vmap()/triangular_solve | solution.py:71
  326.3 46.9 %custom-call.42 = f32[4,128,128]{2,1,0:T(8,128)S(1)} custom-call(f32[4,128,128]{2,1,0:T(8,128)S(1)} %cholesky.172), custom_call_target="Cholesky" | custom-call | tf_op jit(solution)/shard_map/while/body/eval_jaxpr/jit(cholesky)/cholesky | solution.py:68
  373.4 39.3 %custom-call.43 = f32[4,1,128,128]{2,3,1,0:T(8,128)S(1)} custom-call(f32[4,1,128,128]{3,2,1,0:T(8,128)S(1)} %select_bitcast_fusion.3), custom_call_target="InvertDiagBlocksLowerTriangular" | custom-call | tf_op jit(solution)/shard_map/while/body/eval_jaxpr/jit(cholesky)/cholesky | solution.py:68
  413.8 46.9 %custom-call.44 = f32[4,128,128]{2,1,0:T(8,128)S(1)} custom-call(f32[4,128,128]{2,1,0:T(8,128)S(1)} %convolution_subtract_fusion.6), custom_call_target="Cholesky" | custom-call | tf_op jit(solution)/shard_map/while/body/eval_jaxpr/jit(cholesky)/cholesky | solution.py:68
  461.3 3.9 while.18
  465.3 78.6 %custom-call.46 = f32[4,2,128,128]{2,3,1,0:T(8,128)S(1)} custom-call(f32[4,2,128,128]{3,2,1,0:T(8,128)S(1)} %bitcast.144), custom_call_target="InvertDiagBlocksLowerTriangular" | custom-call | tf_op jit(solution)/shard_map/while/body/eval_jaxpr/jit(_cho_solve)/vmap()/triangular_solve | solution.py:71
  (148 shorter events, 43.1 us)
Async XLA Ops:
  0.1 8.9 %copy-start.2 = (s32[16]{0:T(128)S(1)}, s32[16]{0:T(128)}, u32[]{:S(2)}) copy-start(s32[16]{0:T(128)} %param.7) | copy-start | bytes 196
  42.5 21.4 %copy-start.3 = (s32[1,16]{1,0:T(1,128)S(1)}, s32[1,16]{1,0:T(1,128)}, u32[]{:S(2)}) copy-start(s32[1,16]{1,0:T(1,128)} %param.6) | copy-start | bytes 196
  44.3 33.2 %all-to-all-start = ((bf16[64,2,512]{2,1,0:T(2,128)(2,1)}), bf16[64,2,512]{2,1,0:T(2,128)(2,1)S(1)}, u32[]{:S(2)}, u32[]{:S(2)}) async-start(bf16[64,2,512]{2,1,0:T(2,128)(2,1)} %reshape.166), calls=%async_computation | async-start | bytes 262144 | tf_op jit(solution)/shard_map/all_to_all | solution.py:41
  321.7 1.2 copy-start
  322.9 1.0 copy-start.1
  547.9 1.2 copy-start
  549.2 1.0 copy-start.1
where the time goes:
time: 552 us; the launch traced here: 550 us
  other arithmetic  435 us (79%)
  local copies, waits for them, and re-layouts  52.2 us (9%)
  starting transfers between devices  19.6 us (4%)
  blocking collectives  16.7 us (3%)
  waiting for transfers between devices  13.6 us (2%)
  matrix products  11.5 us (2%)
    another operation x20, other arithmetic, solve_group(): jnp.linalg.cholesky(auto_part + ridge_term[:, None, None] * jnp.eye(real_...  267 us
    another operation x8, other arithmetic, solve_group(): transfer_t = jax.scipy.linalg.cho_solve((factor, True), cross_part)  158 us
    gather x48, local copies, waits for them, and re-layouts  32.2 us
    all_to_all x1, starting transfers between devices, local(): lax.all_to_all(spectra, 'bin', split_axis=1, concat_axis=4, tiled=True)  19.6 us
    all_gather x1, blocking collectives, local(): references = lax.all_gather(local_refs, 'grp', axis=3, tiled=True)  16.7 us
    all_to_all x1, waiting for transfers between devices, local(): lax.all_to_all(spectra, 'bin', split_axis=1, concat_axis=4, tiled=True)  13.6 us
  transfers between devices with their start and end apart: 1, of which 1 were waited for; matrix products, arithmetic and copies ran while one was open for 0% of the time, Pallas kernels for 0%

commit v1 on v0

--- a/solution.py
+++ b/solution.py
@@ -40,7 +40,8 @@
     spectra = transform(chan_rows, offsets, dft_table, bin_devices)
     channels = lax.all_to_all(spectra, "bin", split_axis=1, concat_axis=4, tiled=True)[:, 0]
     local_refs = jnp.take(channels, ref_index[0], axis=3)
-    references = lax.all_gather(local_refs, "grp", axis=3, tiled=True)
+    repeated = jnp.stack([local_refs] * lax.axis_size("grp"))
+    references = jnp.concatenate(lax.all_to_all(repeated, "grp", 0, 0), axis=3)
     ref_real = references[0]
     ref_imag = references[1]
     ref_blocks = jnp.stack(

time: 552 us -> 544 us (0.986)
  blocking collectives: 16.7 us -> 0 us
    all_gather x1 -> x0, blocking collectives: 16.7 us -> none  [local(): references = lax.all_gather(local_refs, 'grp', axis=3, tiled=True)]
  transfers between devices with their start and end apart: 1 -> 2, of which waited for: 1 -> 2; matrix products, arithmetic and copies ran while one was open for 0% -> 0% of each run, Pallas kernels for 0% -> 0%
where the time goes in v1:
time: 544 us; the launch traced here: 543 us
  other arithmetic  434 us (80%)
  local copies, waits for them, and re-layouts  52.4 us (10%)
  starting transfers between devices  24.8 us (5%)
  waiting for transfers between devices  17.8 us (3%)
  matrix products  11.4 us (2%)
    another operation x20, other arithmetic, solve_group(): jnp.linalg.cholesky(auto_part + ridge_term[:, None, None] * jnp.eye(real_...  267 us
    another operation x8, other arithmetic, solve_group(): transfer_t = jax.scipy.linalg.cho_solve((factor, True), cross_part)  158 us
    gather x48, local copies, waits for them, and re-layouts  30.8 us
    all_to_all x1, starting transfers between devices, local(): lax.all_to_all(spectra, 'bin', split_axis=1, concat_axis=4, tiled=True)  19.6 us
    all_to_all x1, waiting for transfers between devices, local(): lax.all_to_all(spectra, 'bin', split_axis=1, concat_axis=4, tiled=True)  13.6 us
  transfers between devices with their start and end apart: 2, of which 2 were waited for; matrix products, arithmetic and copies ran while one was open for 0% of the time, Pallas kernels for 0%

profile of v1, /device:TPU:1, one launch (start us, length us, event | category | flops | bytes accessed | tf_op | source)
XLA Modules:
  0.0 543.1 jit_solution(13197831088162692127)
XLA Ops:
  0.1 8.9 %multiply_convert_fusion = (bf16[1024,512]{1,0:T(8,128)(2,1)S(1)}, bf16[1024,512]{1,0:T(8,128)(2,1)S(1)}) fusion(f32[1024]{0:T(1024)S(1)} %multiply_subtract_fusion), kind=kLoop, calls=%fused_computation.58 | loop fusion | flops 9961472 | bytes 2101248 | tf_op jit(solution)/shard_map/convert.2
  9.0 30.9 %while.17 = (s32[]{:T(128)}, bf16[4,8704]{1,0:T(4,128)(2,1)}, s32[16,2]{0,1:T(2,128)S(1)}, bf16[16,4,1024]{2,1,0:T(4,128)(2,1)S(1)}, s32[]{:T(128)}) while((s32[]{:T(128)}, bf16[4,8704]{1,0:T(4,128)(2,1)}, s32[16,2]{0,1:T(2,128)S(1)}, bf16[16,4,1024]{2,1,0:T(4,128)(2,1)S(1)}, s32[]{:T(128)}) %tuple.87), condition=%wide.while_cond.1, body=%wide.while_body.1.sunk | while | flops 2 | bytes 16481 | solution.py:24
  9.6 1.3 bitcast_dynamic-update-slice_fusion.4
  11.5 1.3 bitcast_dynamic-update-slice_fusion.4
  13.4 1.3 bitcast_dynamic-update-slice_fusion.4
  15.4 1.3 bitcast_dynamic-update-slice_fusion.4
  17.3 1.3 bitcast_dynamic-update-slice_fusion.4
  19.2 1.3 bitcast_dynamic-update-slice_fusion.4
  21.1 1.3 bitcast_dynamic-update-slice_fusion.4
  23.1 1.3 bitcast_dynamic-update-slice_fusion.4
  25.0 1.3 bitcast_dynamic-update-slice_fusion.4
  26.9 1.3 bitcast_dynamic-update-slice_fusion.4
  28.9 1.3 bitcast_dynamic-update-slice_fusion.4
  30.8 1.3 bitcast_dynamic-update-slice_fusion.4
  32.7 1.3 bitcast_dynamic-update-slice_fusion.4
  38.5 1.4 bitcast_dynamic-update-slice_fusion.4
  41.1 1.8 reshape.177
  42.9 19.6 %all-to-all-start = ((bf16[64,2,512]{2,1,0:T(2,128)(2,1)}), bf16[64,2,512]{2,1,0:T(2,128)(2,1)S(1)}, u32[]{:S(2)}, u32[]{:S(2)}) async-start(bf16[64,2,512]{2,1,0:T(2,128)(2,1)} %reshape.177), calls=%async_computation | async-start | bytes 262144 | tf_op jit(solution)/shard_map/all_to_all | solution.py:41
  62.6 13.6 %all-to-all-done = bf16[64,2,512]{2,1,0:T(2,128)(2,1)S(1)} async-done(((bf16[64,2,512]{2,1,0:T(2,128)(2,1)}), bf16[64,2,512]{2,1,0:T(2,128)(2,1)S(1)}, u32[]{:S(2)}, u32[]{:S(2)}) %all-to-all-start) | async-done | bytes 131104 | tf_op jit(solution)/shard_map/all_to_all | solution.py:41
  79.3 5.2 all-to-all-start.1
  85.4 4.3 all-to-all-done.1
  90.9 452.2 %while.16 = (s32[]{:T(128)}, bf16[2,4,256,256]{3,2,1,0:T(8,128)(2,1)}, s32[2]{0:T(128)S(1)}, bf16[2,8,16,256]{3,2,1,0:T(8,128)(2,1)S(1)}, bf16[2,8,16,256]{3,2,0...) while((s32[]{:T(128)}, ...), condition=%wide.region_6.7_spmd, body=%wide.region_0.6_spmd.sunk | while | flops 1448117248 | bytes 37234176 | solution.py:75
  93.4 46.9 %custom-call.42 = f32[4,128,128]{2,1,0:T(8,128)S(1)} custom-call(f32[4,128,128]{2,1,0:T(8,128)S(1)} %cholesky.172), custom_call_target="Cholesky" | custom-call | tf_op jit(solution)/shard_map/while/body/eval_jaxpr/jit(cholesky)/cholesky | solution.py:69
  140.5 39.3 %custom-call.43 = f32[4,1,128,128]{2,3,1,0:T(8,128)S(1)} custom-call(f32[4,1,128,128]{3,2,1,0:T(8,128)S(1)} %select_bitcast_fusion.3), custom_call_target="InvertDiagBlocksLowerTriangular" | custom-call | tf_op jit(solution)/shard_map/while/body/eval_jaxpr/jit(cholesky)/cholesky | solution.py:69
  180.9 46.9 %custom-call.44 = f32[4,128,128]{2,1,0:T(8,128)S(1)} custom-call(f32[4,128,128]{2,1,0:T(8,128)S(1)} %convolution_subtract_fusion.6), custom_call_target="Cholesky" | custom-call | tf_op jit(solution)/shard_map/while/body/eval_jaxpr/jit(cholesky)/cholesky | solution.py:69
  228.4 3.7 while.18
  232.2 78.6 %custom-call.46 = f32[4,2,128,128]{2,3,1,0:T(8,128)S(1)} custom-call(f32[4,2,128,128]{3,2,1,0:T(8,128)S(1)} %bitcast.144), custom_call_target="InvertDiagBlocksLowerTriangular" | custom-call | tf_op jit(solution)/shard_map/while/body/eval_jaxpr/jit(_cho_solve)/vmap()/triangular_solve | solution.py:72
  319.4 46.9 %custom-call.42 = f32[4,128,128]{2,1,0:T(8,128)S(1)} custom-call(f32[4,128,128]{2,1,0:T(8,128)S(1)} %cholesky.172), custom_call_target="Cholesky" | custom-call | tf_op jit(solution)/shard_map/while/body/eval_jaxpr/jit(cholesky)/cholesky | solution.py:69
  366.5 39.3 %custom-call.43 = f32[4,1,128,128]{2,3,1,0:T(8,128)S(1)} custom-call(f32[4,1,128,128]{3,2,1,0:T(8,128)S(1)} %select_bitcast_fusion.3), custom_call_target="InvertDiagBlocksLowerTriangular" | custom-call | tf_op jit(solution)/shard_map/while/body/eval_jaxpr/jit(cholesky)/cholesky | solution.py:69
  406.9 46.9 %custom-call.44 = f32[4,128,128]{2,1,0:T(8,128)S(1)} custom-call(f32[4,128,128]{2,1,0:T(8,128)S(1)} %convolution_subtract_fusion.6), custom_call_target="Cholesky" | custom-call | tf_op jit(solution)/shard_map/while/body/eval_jaxpr/jit(cholesky)/cholesky | solution.py:69
  454.4 3.7 while.18
  458.2 78.6 %custom-call.46 = f32[4,2,128,128]{2,3,1,0:T(8,128)S(1)} custom-call(f32[4,2,128,128]{3,2,1,0:T(8,128)S(1)} %bitcast.144), custom_call_target="InvertDiagBlocksLowerTriangular" | custom-call | tf_op jit(solution)/shard_map/while/body/eval_jaxpr/jit(_cho_solve)/vmap()/triangular_solve | solution.py:72
  (154 shorter events, 45.3 us)
Async XLA Ops:
  0.1 8.9 %copy-start.2 = (s32[16]{0:T(128)S(1)}, s32[16]{0:T(128)}, u32[]{:S(2)}) copy-start(s32[16]{0:T(128)} %param.7) | copy-start | bytes 196
  41.1 21.4 %copy-start.3 = (s32[1,16]{1,0:T(1,128)S(1)}, s32[1,16]{1,0:T(1,128)}, u32[]{:S(2)}) copy-start(s32[1,16]{1,0:T(1,128)} %param.6) | copy-start | bytes 196
  42.9 33.2 %all-to-all-start = ((bf16[64,2,512]{2,1,0:T(2,128)(2,1)}), bf16[64,2,512]{2,1,0:T(2,128)(2,1)S(1)}, u32[]{:S(2)}, u32[]{:S(2)}) async-start(bf16[64,2,512]{2,1,0:T(2,128)(2,1)} %reshape.177), calls=%async_computation | async-start | bytes 262144 | tf_op jit(solution)/shard_map/all_to_all | solution.py:41
  79.3 10.4 %all-to-all-start.1 = ((bf16[8,2,2048]{2,1,0:T(2,128)(2,1)}), bf16[8,2,2048]{2,1,0:T(2,128)(2,1)S(1)}, u32[]{:S(2)}, u32[]{:S(2)}) async-start(bf16[8,2,2048]{2,1,0:T(2,128)(2,1)} %reshape.179), calls=%async_computation.1 | async-start | bytes 131072 | tf_op jit(solution)/shard_map/all_to_all | solution.py:44
  314.9 1.2 copy-start
  316.1 1.0 copy-start.1
  540.8 1.2 copy-start
  542.1 1.0 copy-start.1
